TPU v7x, 256 devices: a whole 4x4x8 slice. The times are simulated.
256 devices in a mesh: pole: 4 (over y), row: 8 (over z_lo, x), col: 8 (over z_hi, core).
Axes of the slice: x: 4, y: 4, z: 8 (z_hi: 4, z_lo: 2; z = z_hi * 2 + z_lo), core: 2. Of those that a mesh axis runs over, the one named last changes fastest.
Arguments:
- found_inverse: bfloat16 [4, 2, 8192, 8, 8, 128], P('pole', None, 'row', None, 'col'), may hold values from -0.125 to 0.125
- l_panel: bfloat16 [4, 2, 8192, 512], P('pole', None, ('row', 'col')), may hold values from -1.5 to 1.5
- block_pattern: int32 [64, 4], P(('row', 'col')), may hold values 0 or 1
- sup_widths: int32 [4], replicated, may hold values from 1 to 128, 320 in all
- diag_inverse: bfloat16 [4, 2, 512, 128], P('pole'), may hold values from -6 to 6
- pole_weights: float32 [4, 2], P('pole'), may hold values from -4 to 4
Outputs:
- density: float32 [512, 8192], P('col', 'row')
- diagonal: float32 [512, 128], replicated
Inputs may be any that keep to these rules, and one draw needn't show every extreme that they name: `sup_widths`: one supernode has exactly 128 columns.
All inputs are finite; a program needn't handle non-finite values. No bound on the sum of `block_pattern` on one device may be relied on, other than what follows from the above.
Results may differ from a plain program's by a relative error of at most 0.0003.
Values may be sent and summed in bfloat16 or wider, within the bound.
A program may use at most 128 MiB of HBM per device.

v0:
```python
import jax
import jax.numpy as jnp
from jax import lax
from jax.sharding import PartitionSpec as P


def contract(left, right):
    return jnp.einsum("jk,ij->ki", left, right, preferred_element_type=jnp.float32)


def pair_product(left, right):
    return jnp.einsum("ika,kbi->kab", left, right, precision=lax.Precision.HIGHEST)


def per_device(found_inverse, l_panel, block_pattern, sup_widths, diag_inverse, pole_weights):
    slot_width = diag_inverse.shape[-1]
    total_cols = l_panel.shape[-1]
    supernodes = total_cols // slot_width
    row_count = lax.axis_size("row")
    col_count = lax.axis_size("col")
    row_index = lax.axis_index("row")
    col_index = lax.axis_index("col")
    columns = jnp.arange(total_cols, dtype=jnp.int32)
    column_ok = columns % slot_width < jnp.repeat(sup_widths, slot_width)
    block_ok = jnp.repeat(block_pattern[0], slot_width) == 1
    masked = jnp.where(
        (column_ok & block_ok)[None, None, :], l_panel[0], jnp.zeros((), jnp.bfloat16)
    )
    everything = lax.all_gather(masked, ("row", "col"), axis=1, tiled=True)
    own_rows = lax.dynamic_slice_in_dim(
        everything, row_index * col_count * slot_width, col_count * slot_width, 1
    )
    grouped = everything.reshape(2, row_count, col_count, slot_width, total_cols)
    picked = lax.dynamic_index_in_dim(grouped, col_index, 2, keepdims=False)
    column_rows = picked.reshape(2, row_count * slot_width, total_cols)
    local_rows = found_inverse.shape[2]
    inverse = found_inverse[0].reshape(2, local_rows, row_count * slot_width)
    part_real = contract(column_rows[1], inverse[1]) - contract(column_rows[0], inverse[0])
    part_imag = -(contract(column_rows[1], inverse[0]) + contract(column_rows[0], inverse[1]))
    w_real = pole_weights[0, 0]
    w_imag = pole_weights[0, 1]
    weighted = w_real * part_real - w_imag * part_imag
    whole = lax.psum(weighted, "pole")
    density = lax.psum_scatter(whole, "col", scatter_dimension=0, tiled=True)
    lifted = own_rows.astype(jnp.float32).reshape(2, local_rows, supernodes, slot_width)
    upper_real = part_real.reshape(supernodes, slot_width, local_rows)
    upper_imag = part_imag.reshape(supernodes, slot_width, local_rows)
    t_real = pair_product(lifted[0], upper_real) - pair_product(lifted[1], upper_imag)
    t_imag = pair_product(lifted[0], upper_imag) + pair_product(lifted[1], upper_real)
    lead_flag = ((row_index == 0) & (col_index == 0)).astype(jnp.float32)
    d_real = diag_inverse[0, 0].astype(jnp.float32).reshape(supernodes, slot_width, slot_width)
    d_imag = diag_inverse[0, 1].astype(jnp.float32).reshape(supernodes, slot_width, slot_width)
    local_term = lead_flag * (w_real * d_real - w_imag * d_imag) - (
        w_real * t_real - w_imag * t_imag
    )
    diagonal = lax.psum(local_term.reshape(total_cols, slot_width), ("pole", "row", "col"))
    return (density, diagonal)


def solution(mesh):
    in_specs = (
        P("pole", None, "row", None, "col", None),
        P("pole", None, ("row", "col"), None),
        P(("row", "col"), None),
        P(),
        P("pole", None, None, None),
        P("pole", None),
    )
    out_specs = (P("col", "row"), P())
    return jax.shard_map(
        per_device, mesh=mesh, in_specs=in_specs, out_specs=out_specs, check_vma=False
    )
```

profile of v0, /device:TPU:2, one launch (start us, length us, event | category | flops | bytes accessed | tf_op | source)
XLA Modules:
  0.0 514.2 jit_solution(14721515015720495059)
XLA Ops:
  7.9 0.7 fusion.25
  8.6 1.7 bitcast_select_fusion
  10.4 1.3 fusion.27
  11.7 3.8 fusion.26
  15.5 127.3 %all-gather.2.cloned.1.call-done = bf16[2,8192,512]{2,1,0:T(8,128)(2,1)} async-done(((bf16[2,128,512]{2,1,0:T(8,128)(2,1)}), bf16[2,8192,512]{2,1,0:T(8,128)(2,1)}) %all-gather.2.cloned.1.call-update) | async-done | bytes 16777232 | tf_op jit(solution)/shard_map/all_gather | solution.py:29
  142.8 1.7 constant_dynamic-slice_fusion.3
  144.6 1.3 fusion
  145.9 1.3 fusion.2
  147.5 1.3 fusion.12
  148.8 4.6 multiply_subtract_fusion
  153.4 0.9 copy-done.3
  154.3 1.3 subtract_multiply_fusion
  155.6 3.0 constant_dynamic-slice_fusion.2
  158.6 1.5 copy.9
  160.1 2.3 copy.8
  162.3 3.3 fusion.29
  165.7 1.2 fusion.28
  167.3 1.9 fusion.20
  169.1 2.5 fusion.19
  171.7 25.0 %reduce-scatter.2.cloned.1.call-done = f32[64,1024]{1,0:T(8,128)} async-done(((f32[512,1024]{1,0:T(8,128)}), f32[64,1024]{1,0:T(8,128)}) %reduce-scatter.2.cloned.1.call-update) | async-done | bytes 262160 | tf_op jit(solution)/shard_map/reduce_scatter | solution.py:44
  196.7 259.6 %all-reduce.3.cloned.1.call-done = f32[512,128]{1,0:T(8,128)} async-done(((f32[512,128]{1,0:T(8,128)}), f32[512,128]{1,0:T(8,128)}) %all-reduce.3.cloned.1.call-update) | async-done | bytes 262160 | tf_op jit(solution)/shard_map/psum | solution.py:56
  456.3 48.0 %all-reduce.5.cloned.1.call-done = f32[64,1024]{1,0:T(8,128)} async-done(((f32[64,1024]{1,0:T(8,128)}), f32[64,1024]{1,0:T(8,128)}) %all-reduce.5.cloned.1.call-update) | async-done | bytes 262160 | tf_op jit(solution)/shard_map/psum | solution.py:43
  504.3 1.7 copy.36
  506.0 1.7 copy.37
  (16 shorter events, 1.5 us)
Async XLA Ops:
  7.2 135.7 %all-gather.2.cloned.1.call-start = ((), (), s32[]{:S(2)}) async-start(), calls=%async_computation.1 | async-start | bytes 17039360 | tf_op jit(solution)/shard_map/all_gather | solution.py:29
  10.3 186.4 %reduce-scatter.2.cloned.1.call-start = ((), (), s32[]{:S(2)}) async-start(), calls=%async_computation.3 | async-start | bytes 2359296 | tf_op jit(solution)/shard_map/reduce_scatter | solution.py:44
  145.9 1.6 copy-start.2
  153.4 0.9 copy-start.3
  153.4 302.9 %all-reduce.3.cloned.1.call-start = ((), (), s32[]{:S(2)}) async-start(), calls=%async_computation.2 | async-start | bytes 524288 | tf_op jit(solution)/shard_map/psum | solution.py:56
  162.3 3.3 copy-start.1
  165.7 1.6 copy-start
  171.6 332.7 %all-reduce.5.cloned.1.call-start = ((), (), s32[]{:S(2)}) async-start(), calls=%async_computation.4 | async-start | bytes 524288 | tf_op jit(solution)/shard_map/psum | solution.py:43
Sparse Core Ops, SparseCore 0:
  10.4 132.3 all-gather.1
  153.5 43.1 reduce-scatter.1
  202.7 253.5 all-reduce.2
  458.5 45.7 all-reduce.4
where the time goes:
time: 515 us; the launch traced here: 514 us
  waiting for transfers between devices  460 us (89%)
  local copies, waits for them, and re-layouts  18.5 us (4%)
  matrix products  17.3 us (3%)
  between operations  13.9 us (3%)
    psum x1, waiting for transfers between devices, per_device(): lax.psum(local_term.reshape(total_cols, slot_width), ('pole', 'row', 'col'))  260 us
    all_gather x1, waiting for transfers between devices, per_device(): everything = lax.all_gather(masked, ('row', 'col'), axis=1, tiled=True)  127 us
    psum x1, waiting for transfers between devices, per_device(): whole = lax.psum(weighted, 'pole')  48 us
    reduce_scatter x1, waiting for transfers between devices, per_device(): density = lax.psum_scatter(whole, 'col', scatter_dimension=0, tiled=True)  25 us
  transfers between devices with their start and end apart: 4, of which 4 were waited for; matrix products, arithmetic and copies ran while one was open for 4% of the time, Pallas kernels for 0%

commit v1 on v0

--- a/solution.py
+++ b/solution.py
@@ -40,7 +40,7 @@
     w_real = pole_weights[0, 0]
     w_imag = pole_weights[0, 1]
     weighted = w_real * part_real - w_imag * part_imag
-    whole = lax.psum(weighted, "pole")
+    whole = jnp.sum(lax.all_gather(weighted, "pole"), axis=0)
     density = lax.psum_scatter(whole, "col", scatter_dimension=0, tiled=True)
     lifted = own_rows.astype(jnp.float32).reshape(2, local_rows, supernodes, slot_width)
     upper_real = part_real.reshape(supernodes, slot_width, local_rows)

time: 515 us -> 554 us (1.076)
  waiting for transfers between devices: 460 us -> 495 us
  other arithmetic: 4.33 us -> 10.3 us
    all_gather x0 -> x1, waiting for transfers between devices: none -> 65.8 us  [per_device(): whole = jnp.sum(lax.all_gather(weighted, 'pole'), axis=0)]
    psum x1 -> x0, waiting for transfers between devices: 48 us -> none  [per_device(): whole = lax.psum(weighted, 'pole')]
    reduce_scatter x1, waiting for transfers between devices: 25 us -> 46 us  [per_device(): density = lax.psum_scatter(whole, 'col', scatter_dimension=0, tiled=True)]
    reduce_sum x0 -> x1, other arithmetic: none -> 5.9 us  [per_device(): whole = jnp.sum(lax.all_gather(weighted, 'pole'), axis=0)]
  transfers between devices with their start and end apart: 4 -> 4, of which waited for: 4 -> 4; matrix products, arithmetic and copies ran while one was open for 4% -> 5% of each run, Pallas kernels for 0% -> 0%
where the time goes in v1:
time: 554 us
  waiting for transfers between devices  495 us (89%)
  matrix products  17.7 us (3%)
  local copies, waits for them, and re-layouts  17.2 us (3%)
  between operations  13.9 us (3%)
  other arithmetic  10.3 us (2%)
    psum x1, waiting for transfers between devices, per_device(): lax.psum(local_term.reshape(total_cols, slot_width), ('pole', 'row', 'col'))  255 us
    all_gather x1, waiting for transfers between devices, per_device(): everything = lax.all_gather(masked, ('row', 'col'), axis=1, tiled=True)  127 us
    all_gather x1, waiting for transfers between devices, per_device(): whole = jnp.sum(lax.all_gather(weighted, 'pole'), axis=0)  65.8 us
    reduce_scatter x1, waiting for transfers between devices, per_device(): density = lax.psum_scatter(whole, 'col', scatter_dimension=0, tiled=True)  46 us
  transfers between devices with their start and end apart: 4, of which 4 were waited for; matrix products, arithmetic and copies ran while one was open for 5% of the time, Pallas kernels for 0%

profile of v1, /device:TPU:2, one launch (start us, length us, event | category | flops | bytes accessed | tf_op | source)
XLA Modules:
  0.0 553.9 jit_solution(6989651585026230357)
XLA Ops:
  7.9 0.7 fusion.25
  8.6 1.7 bitcast_select_fusion
  10.4 1.4 fusion.27
  11.7 3.8 fusion.26
  15.6 127.3 %all-gather.4.cloned.1.call-done = bf16[2,8192,512]{2,1,0:T(8,128)(2,1)} async-done(((bf16[2,128,512]{2,1,0:T(8,128)(2,1)}), bf16[2,8192,512]{2,1,0:T(8,128)(2,1)}) %all-gather.4.cloned.1.call-update) | async-done | bytes 16777232 | tf_op jit(solution)/shard_map/all_gather | solution.py:29
  142.8 1.7 constant_dynamic-slice_fusion.3
  144.6 1.3 fusion
  145.9 1.3 fusion.2
  147.5 1.3 fusion.12
  148.8 4.7 multiply_subtract_fusion
  153.5 0.9 copy-done.3
  154.4 1.3 subtract_multiply_fusion
  155.8 3.1 constant_dynamic-slice_fusion.2
  158.8 1.5 copy.9
  160.3 2.3 copy.8
  162.6 3.5 fusion.29
  166.1 1.2 fusion.28
  168.0 1.9 fusion.20
  169.8 2.5 fusion.19
  172.4 65.8 %all-gather.6.cloned.1.call-done = f32[2048,1024]{1,0:T(8,128)} async-done(((f32[512,1024]{1,0:T(8,128)}), f32[2048,1024]{1,0:T(8,128)}) %all-gather.6.cloned.1.call-update) | async-done | bytes 8388624 | tf_op jit(solution)/shard_map/all_gather | solution.py:43
  238.2 5.9 %reduce_sum.9 = f32[512,1024]{1,0:T(8,128)} reduce(f32[4,512,1024]{2,1,0:T(8,128)} %bitcast.64, f32[]{:T(128)} %constant.36.clone.1), dimensions={0}, to_apply=%region_0.1 | reduce | flops 1572864 | bytes 10485764 | tf_op jit(solution)/shard_map/reduce_sum | solution.py:43
  244.2 255.4 %all-reduce.2.cloned.1.call-done = f32[512,128]{1,0:T(8,128)} async-done(((f32[512,128]{1,0:T(8,128)}), f32[512,128]{1,0:T(8,128)}) %all-reduce.2.cloned.1.call-update) | async-done | bytes 262160 | tf_op jit(solution)/shard_map/psum | solution.py:56
  499.6 46.0 %reduce-scatter.2.cloned.1.call-done = f32[64,1024]{1,0:T(8,128)} async-done(((f32[512,1024]{1,0:T(8,128)}), f32[64,1024]{1,0:T(8,128)}) %reduce-scatter.2.cloned.1.call-update) | async-done | bytes 262160 | tf_op jit(solution)/shard_map/reduce_scatter | solution.py:44
  545.7 1.7 copy.35
  (16 shorter events, 1.8 us)
Async XLA Ops:
  7.2 135.7 %all-gather.4.cloned.1.call-start = ((), (), s32[]{:S(2)}) async-start(), calls=%async_computation.1 | async-start | bytes 17039360 | tf_op jit(solution)/shard_map/all_gather | solution.py:29
  10.3 227.9 %all-gather.6.cloned.1.call-start = ((), (), s32[]{:S(2)}) async-start(), calls=%async_computation.4 | async-start | bytes 10485760 | tf_op jit(solution)/shard_map/all_gather | solution.py:43
  145.9 1.6 copy-start.2
  153.5 0.9 copy-start.3
  153.5 346.1 %all-reduce.2.cloned.1.call-start = ((), (), s32[]{:S(2)}) async-start(), calls=%async_computation.3 | async-start | bytes 524288 | tf_op jit(solution)/shard_map/psum | solution.py:56
  162.6 3.5 copy-start.1
  166.1 1.9 copy-start
  172.4 373.3 %reduce-scatter.2.cloned.1.call-start = ((), (), s32[]{:S(2)}) async-start(), calls=%async_computation.2 | async-start | bytes 2359296 | tf_op jit(solution)/shard_map/reduce_scatter | solution.py:44
Sparse Core Ops, SparseCore 0:
  10.4 132.3 all-gather.3
  153.6 84.5 all-gather.5
  244.3 255.2 all-reduce.1
  502.6 43.0 reduce-scatter.1

commit v2 on v0

--- a/solution.py
+++ b/solution.py
@@ -53,7 +53,9 @@
     local_term = lead_flag * (w_real * d_real - w_imag * d_imag) - (
         w_real * t_real - w_imag * t_imag
     )
-    diagonal = lax.psum(local_term.reshape(total_cols, slot_width), ("pole", "row", "col"))
+    diagonal = lax.psum(
+        lax.psum(local_term.reshape(total_cols, slot_width), "pole"), ("row", "col")
+    )
     return (density, diagonal)
 
 

time: 515 us -> 440 us (0.85)
  waiting for transfers between devices: 460 us -> 383 us
    psum x1, waiting for transfers between devices: 260 us -> 180 us  [per_device(): lax.psum(lax.psum(local_term.reshape(total_cols, slot_width), 'pole'), ('...]
  transfers between devices with their start and end apart: 4 -> 4, of which waited for: 4 -> 4; matrix products, arithmetic and copies ran while one was open for 4% -> 5% of each run, Pallas kernels for 0% -> 0%
where the time goes in v2:
time: 440 us; the launch traced here: 437 us
  waiting for transfers between devices  383 us (87%)
  local copies, waits for them, and re-layouts  18.5 us (4%)
  matrix products  17.4 us (4%)
  between operations  13.9 us (3%)
    psum x1, waiting for transfers between devices, per_device(): lax.psum(lax.psum(local_term.reshape(total_cols, slot_width), 'pole'), ('...  180 us
    all_gather x1, waiting for transfers between devices, per_device(): everything = lax.all_gather(masked, ('row', 'col'), axis=1, tiled=True)  127 us
    psum x1, waiting for transfers between devices, per_device(): whole = lax.psum(weighted, 'pole')  51.1 us
    reduce_scatter x1, waiting for transfers between devices, per_device(): density = lax.psum_scatter(whole, 'col', scatter_dimension=0, tiled=True)  24.3 us
    dot_general x4, matrix products, pair_product(): jnp.einsum('ika,kbi->kab', left, right, precision=lax.Precision.HIGHEST)  8.91 us
  transfers between devices with their start and end apart: 4, of which 4 were waited for; matrix products, arithmetic and copies ran while one was open for 5% of the time, Pallas kernels for 0%

profile of v2, /device:TPU:2, one launch (start us, length us, event | category | flops | bytes accessed | tf_op | source)
XLA Modules:
  0.0 437.3 jit_solution(10545760611642574836)
XLA Ops:
  7.9 0.7 fusion.25
  8.6 1.7 bitcast_select_fusion
  10.4 1.4 fusion.27
  11.7 3.8 fusion.26
  15.5 127.3 %all-gather.2.cloned.1.call-done = bf16[2,8192,512]{2,1,0:T(8,128)(2,1)} async-done(((bf16[2,128,512]{2,1,0:T(8,128)(2,1)}), bf16[2,8192,512]{2,1,0:T(8,128)(2,1)}) %all-gather.2.cloned.1.call-update) | async-done | bytes 16777232 | tf_op jit(solution)/shard_map/all_gather | solution.py:29
  142.8 1.7 constant_dynamic-slice_fusion.3
  144.6 1.3 fusion
  145.9 1.3 fusion.2
  147.5 1.3 fusion.12
  148.8 4.6 %multiply_subtract_fusion = (f32[512,1024]{1,0:T(8,128)}, f32[512,1024]{1,0:T(8,128)}) fusion(f32[512,1024]{1,0:T(8,128)S(1)} %fusion.12, f32[]{:T(128)} %bitcast.8, f32[]{:T(128)} %bitcast, f32[512,1024]{1,0:T(8,128)S(1)} %fusion, bf16[1024,512]{1,0:T(8,128)(2,1)S(1)} %bitcast.66, bf16[128,8,8,128]{3,2,1,0:T(8,128)(2,1)S(1)} %bitcast.64), kind=kOutput, calls=%fused_computation.8 | convolution fusion | flops 1076363264 | bytes 11534344 | tf_op jit(solution)/shard_map/jk,ij->ki/dot_general | solution.py:8
  153.5 0.9 copy-done.3
  154.4 1.3 subtract_multiply_fusion
  155.7 3.0 constant_dynamic-slice_fusion.2
  158.7 1.5 copy.9
  160.2 2.3 copy.8
  162.5 3.3 fusion.29
  165.8 1.2 fusion.28
  167.4 1.9 fusion.20
  169.2 2.5 fusion.19
  171.8 24.3 %reduce-scatter.2.cloned.1.call-done = f32[64,1024]{1,0:T(8,128)} async-done(((f32[512,1024]{1,0:T(8,128)}), f32[64,1024]{1,0:T(8,128)}) %reduce-scatter.2.cloned.1.call-update) | async-done | bytes 262160 | tf_op jit(solution)/shard_map/reduce_scatter | solution.py:44
  196.1 51.1 %all-reduce.6.cloned.1.call-done = (f32[64,1024]{1,0:T(8,128)}, f32[512,128]{1,0:T(8,128)}) async-done(((f32[64,1024]{1,0:T(8,128)}, f32[512,128]{1,0:T(8,128)}), (f32[64,1024]{1,0:T(8,128)}, f32[512,128]{1,0:T(8,128)})) %all-reduce.6.cloned.1.call-update) | async-done | bytes 524304 | tf_op jit(solution)/shard_map/psum | solution.py:43
  247.2 180.2 %all-reduce.4.cloned.1.call-done = f32[512,128]{1,0:T(8,128)} async-done(((f32[512,128]{1,0:T(8,128)}), f32[512,128]{1,0:T(8,128)}) %all-reduce.4.cloned.1.call-update) | async-done | bytes 262160 | tf_op jit(solution)/shard_map/psum | solution.py:56
  427.4 1.7 copy.37
  429.1 1.7 copy.38
  (16 shorter events, 1.5 us)
Async XLA Ops:
  7.2 135.7 %all-gather.2.cloned.1.call-start = ((), (), s32[]{:S(2)}) async-start(), calls=%async_computation.1 | async-start | bytes 17039360 | tf_op jit(solution)/shard_map/all_gather | solution.py:29
  10.3 185.7 %reduce-scatter.2.cloned.1.call-start = ((), (), s32[]{:S(2)}) async-start(), calls=%async_computation.3 | async-start | bytes 2359296 | tf_op jit(solution)/shard_map/reduce_scatter | solution.py:44
  145.9 1.6 copy-start.2
  153.4 0.9 copy-start.3
  153.4 93.8 %all-reduce.6.cloned.1.call-start = ((), (), s32[]{:S(2)}) async-start(), calls=%async_computation.4 | async-start | bytes 1048576 | tf_op jit(solution)/shard_map/psum | solution.py:43
  162.5 3.4 copy-start.1
  165.8 1.6 copy-start
  196.1 231.3 %all-reduce.4.cloned.1.call-start = ((), (), s32[]{:S(2)}) async-start(), calls=%async_computation.2 | async-start | bytes 524288 | tf_op jit(solution)/shard_map/psum | solution.py:56
Sparse Core Ops, SparseCore 0:
  10.4 132.3 all-gather.1
  153.6 42.4 reduce-scatter.1
  199.0 48.1 all-reduce.5
  250.5 176.7 all-reduce.3

commit v3 on v0

--- a/solution.py
+++ b/solution.py
@@ -26,7 +26,10 @@
     masked = jnp.where(
         (column_ok & block_ok)[None, None, :], l_panel[0], jnp.zeros((), jnp.bfloat16)
     )
-    everything = lax.all_gather(masked, ("row", "col"), axis=1, tiled=True)
+    everything = jnp.concatenate(
+        lax.all_to_all(jnp.stack([masked] * lax.axis_size(("row", "col"))), ("row", "col"), 0, 0),
+        axis=1,
+    )
     own_rows = lax.dynamic_slice_in_dim(
         everything, row_index * col_count * slot_width, col_count * slot_width, 1
     )

time: 515 us -> 746 us (1.45)
  waiting for transfers between devices: 460 us -> 665 us
  local copies, waits for them, and re-layouts: 18.5 us -> 32 us
  starting transfers between devices: 0.16 us -> 12.6 us
    all_to_all x0 -> x1, waiting for transfers between devices: none -> 359 us  [per_device(): lax.all_to_all(jnp.stack([masked] * lax.axis_size(('row', 'col'))), ('row...]
    all_gather x1 -> x0, waiting for transfers between devices: 127 us -> none  [per_device(): everything = lax.all_gather(masked, ('row', 'col'), axis=1, tiled=True)]
    psum x1, waiting for transfers between devices: 260 us -> 227 us  [per_device(): lax.psum(local_term.reshape(total_cols, slot_width), ('pole', 'row', 'col'))]
    all_to_all x0 -> x1, starting transfers between devices: none -> 12.3 us  [per_device(): lax.all_to_all(jnp.stack([masked] * lax.axis_size(('row', 'col'))), ('row...]
    all_to_all x0 -> x1, local copies, waits for them, and re-layouts: none -> 8.48 us  [per_device(): lax.all_to_all(jnp.stack([masked] * lax.axis_size(('row', 'col'))), ('row...]
  transfers between devices with their start and end apart: 4 -> 4, of which waited for: 4 -> 4; matrix products, arithmetic and copies ran while one was open for 4% -> 3% of each run, Pallas kernels for 0% -> 0%
where the time goes in v3:
time: 746 us; the launch traced here: 745 us
  waiting for transfers between devices  665 us (89%)
  local copies, waits for them, and re-layouts  32 us (4%)
  matrix products  16.7 us (2%)
  between operations  15.6 us (2%)
  starting transfers between devices  12.6 us (2%)
    all_to_all x1, waiting for transfers between devices, per_device(): lax.all_to_all(jnp.stack([masked] * lax.axis_size(('row', 'col'))), ('row...  359 us
    psum x1, waiting for transfers between devices, per_device(): lax.psum(local_term.reshape(total_cols, slot_width), ('pole', 'row', 'col'))  227 us
    psum x1, waiting for transfers between devices, per_device(): whole = lax.psum(weighted, 'pole')  47.8 us
    reduce_scatter x1, waiting for transfers between devices, per_device(): density = lax.psum_scatter(whole, 'col', scatter_dimension=0, tiled=True)  31 us
  transfers between devices with their start and end apart: 4, of which 4 were waited for; matrix products, arithmetic and copies ran while one was open for 3% of the time, Pallas kernels for 0%

profile of v3, /device:TPU:2, one launch (start us, length us, event | category | flops | bytes accessed | tf_op | source)
XLA Modules:
  0.0 745.4 jit_solution(6149802220030964391)
XLA Ops:
  9.4 1.0 select_bitcast_fusion
  10.4 6.0 stack.5
  16.3 12.3 %all-to-all-start = ((bf16[64,2,128,512]{3,2,1,0:T(8,128)(2,1)}), bf16[64,2,128,512]{3,2,1,0:T(8,128)(2,1)}, u32[]{:S(2)}, u32[]{:S(2)}) async-start(bf16[64,2,128,512]{3,2,1,0:T(8,128)(2,1)} %stack.5), calls=%async_computation | async-start | bytes 33554432 | tf_op jit(solution)/shard_map/all_to_all | solution.py:30
  29.3 3.8 fusion.26
  33.1 358.7 %all-to-all-done = bf16[64,2,128,512]{3,2,1,0:T(8,128)(2,1)} async-done(((bf16[64,2,128,512]{3,2,1,0:T(8,128)(2,1)}), bf16[64,2,128,512]{3,2,1,0:T(8,128)(2,1)}, u32[]{:S(2)}, u32[]{:S(2)}) %all-to-all-start) | async-done | bytes 16777248 | tf_op jit(solution)/shard_map/all_to_all | solution.py:30
  391.8 8.5 %copy.11 = bf16[64,2,128,512]{3,2,0,1:T(8,128)(2,1)S(1)} copy(bf16[64,2,128,512]{3,2,1,0:T(8,128)(2,1)} %all-to-all-done) | data formatting | bytes 33554432 | tf_op jit(solution)/shard_map/all_to_all | solution.py:30
  400.6 1.3 fusion.2
  401.9 1.3 fusion
  403.2 3.5 copy-done
  406.6 1.3 fusion.12
  408.0 4.7 multiply_subtract_fusion
  413.6 1.3 subtract_multiply_fusion
  414.9 2.6 constant_dynamic-slice_fusion.2
  417.6 1.3 copy.14
  418.9 1.5 copy.15
  420.4 2.5 fusion.28
  423.0 1.2 fusion.29
  424.1 1.9 fusion.20
  426.0 2.5 fusion.19
  428.6 31.0 %reduce-scatter.2.cloned.1.call-done = f32[64,1024]{1,0:T(8,128)} async-done(((f32[512,1024]{1,0:T(8,128)}), f32[64,1024]{1,0:T(8,128)}) %reduce-scatter.2.cloned.1.call-update) | async-done | bytes 262160 | tf_op jit(solution)/shard_map/reduce_scatter | solution.py:47
  459.7 227.1 %all-reduce.3.cloned.1.call-done = f32[512,128]{1,0:T(8,128)} async-done(((f32[512,128]{1,0:T(8,128)}), f32[512,128]{1,0:T(8,128)}) %all-reduce.3.cloned.1.call-update) | async-done | bytes 262160 | tf_op jit(solution)/shard_map/psum | solution.py:59
  686.8 47.8 %all-reduce.5.cloned.1.call-done = f32[64,1024]{1,0:T(8,128)} async-done(((f32[64,1024]{1,0:T(8,128)}), f32[64,1024]{1,0:T(8,128)}) %all-reduce.5.cloned.1.call-update) | async-done | bytes 262160 | tf_op jit(solution)/shard_map/psum | solution.py:46
  734.6 1.7 copy.42
  736.3 1.7 copy.43
  (21 shorter events, 3.2 us)
Async XLA Ops:
  16.3 12.4 %copy-start.5 = (f32[1,2]{1,0:T(1,128)S(1)}, f32[1,2]{1,0:T(1,128)}, u32[]{:S(2)}) copy-start(f32[1,2]{1,0:T(1,128)} %param.11) | copy-start | bytes 28
  16.3 375.5 %all-to-all-start = ((bf16[64,2,128,512]{3,2,1,0:T(8,128)(2,1)}), bf16[64,2,128,512]{3,2,1,0:T(8,128)(2,1)}, u32[]{:S(2)}, u32[]{:S(2)}) async-start(bf16[64,2,128,512]{3,2,1,0:T(8,128)(2,1)} %stack.5), calls=%async_computation | async-start | bytes 33554432 | tf_op jit(solution)/shard_map/all_to_all | solution.py:30
  28.7 431.0 %reduce-scatter.2.cloned.1.call-start = ((), (), s32[]{:S(2)}) async-start(), calls=%async_computation.3 | async-start | bytes 2359296 | tf_op jit(solution)/shard_map/reduce_scatter | solution.py:47
  400.3 6.3 copy-start
  401.9 4.8 copy-start.3
  412.6 0.9 copy-start.4
  412.6 274.1 %all-reduce.3.cloned.1.call-start = ((), (), s32[]{:S(2)}) async-start(), calls=%async_computation.2 | async-start | bytes 524288 | tf_op jit(solution)/shard_map/psum | solution.py:59
  420.4 2.6 copy-start.1
  420.4 2.6 copy-start.2
  428.6 306.0 %all-reduce.5.cloned.1.call-start = ((), (), s32[]{:S(2)}) async-start(), calls=%async_computation.4 | async-start | bytes 524288 | tf_op jit(solution)/shard_map/psum | solution.py:46
Sparse Core Ops, SparseCore 0:
  412.8 46.8 reduce-scatter.1
Sparse Core Ops, SparseCore 1:
  428.7 258.1 all-reduce.2
  689.0 45.6 all-reduce.4
